TPU v7x, 32 devices: a whole 2x2x4 slice. The times are simulated.
32 devices in a mesh: tiles: 8 (over z, x), chan: 4 (over y, core).
Axes of the slice: x: 2, y: 2, z: 4, core: 2. Of those that a mesh axis runs over, the one named last changes fastest.
Arguments:
- features: bfloat16 [512, 64, 256], P('tiles'), may hold values from -6 to 6
- weights: bfloat16 [27, 256, 256], P(None, None, 'chan')
- gain: bfloat16 [256], P('chan'), may hold values from 0.099609375 to 1.8984375
- rulebook: int32 [6144, 4], P('tiles'), may hold values from 0 to 191, as said below
- recv_list: int32 [8, 128], P('tiles'), may hold values from 0 to 63, as said below
- coarse_send: int32 [8, 8], P('tiles'), may hold values from 0 to 7, as said below
- coarse_place: int32 [8, 8], P('tiles'), may hold values from 0 to 7, as said below
Outputs:
- skip_features: bfloat16 [512, 64, 256], P('tiles', None, 'chan')
- coarse_features: bfloat16 [64, 64, 256], P('tiles', None, 'chan')
Inputs may be any that keep to these rules, and one draw needn't show every extreme that they name: `rulebook`: Columns: input tile 0 to 63 of the device; kernel offset 0 to 26, or 27 for an empty row; direction 0 to 26, the input tile's place relative to the output tile, along each dimension 0 or equal to the kernel offset's nonzero component; target below 64 a tile of the device, else slot s = target - 64 for device d + dist(s // 16), which always exists. Empty rows have 0 in the other columns and direction 13. Each device has 192 or more live rows, some device none empty; every slot toward an existing device is named by a live row, and every tile has a row with offset 13, direction 13 and itself as input and target. `recv_list`: each tile of a device is named exactly twice in its row. `coarse_send`: strided owner map: coarse tile k of device s, global number p = s * 8 + k, goes to an owner that depends only on p % 8 (a permutation of the devices), in lane k // 8; slots of one row are distinct. `coarse_place`: the slot s + j of owner e holds the place of the coarse tile it receives; 8 marks a slot that carries nothing. Every coarse tile of the owner is written by exactly one slot.
All inputs are finite; a program needn't handle non-finite values.
Results may differ from a plain program's by a relative error of at most 0.0045.
Values may be sent and summed in bfloat16 or wider, within the bound.
No kernel may reach another device: no remote copies, remote signals or barrier semaphores. Data moves between devices by JAX's collectives and lax.ppermute only.
A program may use at most 128 MiB of HBM per device.

v0:
```python
import jax
import jax.numpy as jnp
from jax import lax
from jax.sharding import PartitionSpec as P

epsilon = 1e-05


def from_behind(block, axis, distance):
    devices = range(lax.axis_size(axis))
    route = [(i - distance, i) for i in devices if i - distance in devices]
    return lax.ppermute(block, axis, route)


def offsets(code):
    return jnp.stack([code // 9 - 1, code // 3 % 3 - 1, code % 3 - 1], axis=-1)


def shift_table(kernel, heading):
    voxel = jnp.arange(64, dtype=jnp.int32)
    corner = jnp.stack([voxel // 16, voxel // 4 % 4, voxel % 4], axis=-1)
    source = (
        corner[None, :, :]
        + offsets(jnp.minimum(kernel, 26))[:, None, :]
        - 4 * offsets(heading)[:, None, :]
    )
    inside = jnp.all((source >= 0) & (source < 4), axis=-1) & (kernel < 27)[:, None]
    source = jnp.clip(source, 0, 3)
    where_from = source[..., 0] * 16 + source[..., 1] * 4 + source[..., 2]
    return (where_from, inside)


def pool_blocks(values):
    dims_in = values.shape
    blocked = values.astype(jnp.float32).reshape(dims_in[:-2] + (2, 2, 2, 2, 2, 2, dims_in[-1]))
    return (
        jnp.mean(blocked, axis=(-6, -4, -2))
        .reshape(dims_in[:-2] + (8, dims_in[-1]))
        .astype(jnp.bfloat16)
    )


def assemble(placed):
    number = placed.shape[0]
    blocked = placed.reshape(number, 2, 2, 2, 2, 2, 2, placed.shape[-1])
    return blocked.transpose(0, 1, 4, 2, 5, 3, 6, 7).reshape(number, 64, placed.shape[-1])


def body(features, weights, gain, rulebook, recv_list, coarse_send, coarse_place):
    tile_count = features.shape[0]
    channels = features.shape[2]
    quarter = weights.shape[2]
    rule_rows = rulebook.shape[0]
    block_rows = min(128, rule_rows)
    slot_width = tile_count // 4
    chan_pos = lax.axis_index("chan")
    own_part = lax.dynamic_slice_in_dim(features, chan_pos * quarter, quarter, 2)
    grouped = rulebook.reshape(rule_rows // block_rows, block_rows, 4)
    voxel = jnp.arange(64, dtype=jnp.int32)
    tile_ids = jnp.arange(tile_count, dtype=jnp.int32)
    target_ids = jnp.arange(3 * tile_count, dtype=jnp.int32)
    flat_features = features.reshape(tile_count, 64 * channels)

    def step_rules(totals, group):
        where_from, inside = shift_table(group[:, 1], group[:, 2])
        picker = ((where_from[:, :, None] == voxel[None, None, :]) & inside[:, :, None]).astype(
            jnp.bfloat16
        )
        source_hot = (group[:, 0][:, None] == tile_ids[None, :]).astype(jnp.bfloat16)
        fetched = jnp.dot(source_hot, flat_features, preferred_element_type=jnp.float32).astype(
            jnp.bfloat16
        )
        fetched = fetched.reshape(group.shape[0], 64, channels)
        chosen = jnp.einsum(
            "bvu,buc->bvc", picker, fetched, preferred_element_type=jnp.float32
        ).astype(jnp.bfloat16)
        kernels = weights[jnp.minimum(group[:, 1], 26)]
        partial_out = jnp.einsum(
            "bvc,bcq->bvq", chosen, kernels, preferred_element_type=jnp.float32
        )
        target_hot = (target_ids[:, None] == group[:, 3][None, :]).astype(jnp.float32)
        added = jnp.dot(
            target_hot,
            partial_out.reshape(group.shape[0], 64 * quarter),
            precision=lax.Precision.HIGHEST,
            preferred_element_type=jnp.float32,
        )
        return (totals + added.reshape(3 * tile_count, 64, quarter), None)

    start = jnp.zeros((3 * tile_count, 64, quarter), jnp.float32)
    totals, unused = lax.scan(step_rules, start, grouped)
    outgoing = totals[tile_count:].astype(jnp.bfloat16).reshape(8, slot_width, 64, quarter)
    arrivals = []
    for group in range(8):
        distance = group + 1 if group < 4 else 3 - group
        arrivals.append(from_behind(outgoing[group], "tiles", distance))
    incoming = jnp.stack(arrivals, axis=0).reshape(2 * tile_count, 64 * quarter)
    receive_hot = (tile_ids[:, None] == recv_list[0][None, :]).astype(jnp.bfloat16)
    gathered_in = jnp.dot(receive_hot, incoming, preferred_element_type=jnp.float32).reshape(
        tile_count, 64, quarter
    )
    convolved = totals[:tile_count] + gathered_in
    squares = lax.psum(jnp.sum(convolved * convolved, axis=-1), "chan")
    mean_square = squares[:, :, None] / channels
    hidden = jax.nn.silu(gain.astype(jnp.float32) * convolved * lax.rsqrt(mean_square + epsilon))
    skip_features = (own_part.astype(jnp.float32) + hidden).astype(jnp.bfloat16)
    pooled = pool_blocks(skip_features)
    parents = assemble(pooled.reshape(tile_count // 8, 8, 8, quarter))
    slot_count = coarse_place.shape[1]
    parent_count = tile_count // 8
    slot_ids = jnp.arange(slot_count, dtype=jnp.int32)
    parent_ids = jnp.arange(parent_count, dtype=jnp.int32)
    send_hot = (slot_ids[:, None] == coarse_send[0][None, :]).astype(jnp.bfloat16)
    outbound = jnp.dot(
        send_hot, parents.reshape(parent_count, 64 * quarter), preferred_element_type=jnp.float32
    ).astype(jnp.bfloat16)
    outbound = outbound.reshape(slot_count, 64, quarter)
    landed = lax.all_to_all(outbound, "tiles", split_axis=0, concat_axis=0, tiled=True)
    place_hot = (parent_ids[:, None] == coarse_place[0][None, :]).astype(jnp.bfloat16)
    coarse_features = jnp.dot(
        place_hot, landed.reshape(slot_count, 64 * quarter), preferred_element_type=jnp.float32
    ).astype(jnp.bfloat16)
    coarse_features = coarse_features.reshape(parent_count, 64, quarter)
    return (skip_features, coarse_features)


def solution(mesh):
    in_specs = (
        P("tiles", None, None),
        P(None, None, "chan"),
        P("chan"),
        P("tiles", None),
        P("tiles", None),
        P("tiles", None),
        P("tiles", None),
    )
    out_specs = (P("tiles", None, "chan"), P("tiles", None, "chan"))
    return jax.shard_map(body, mesh=mesh, in_specs=in_specs, out_specs=out_specs, check_vma=False)
```

profile of v0, /device:TPU:0, one launch (start us, length us, event | category | flops | bytes accessed | tf_op | source)
XLA Modules:
  0.0 264.5 jit_solution(9480351480479693915)
XLA Ops:
  0.7 4.3 %copy.38 = bf16[8,8,64,256]{3,1,2,0:T(8,128)(2,1)} copy(bf16[8,8,64,256]{3,2,1,0:T(8,128)(2,1)} %bitcast.91) | data formatting | bytes 4194304
  4.9 160.6 %while.16 = (s32[]{:T(128)}, f32[192,64,64]{0,2,1:T(8,128)}, s32[6,128,4]{1,2,0:T(4,128)}, bf16[64,16384]{1,0:T(8,128)(2,1)}, bf16[27,256,64]{1,2,0:T(8,128)(2,1)S(1)}, /*index=5*/s32[]{:T(128)}, s32[]{:T(128)}) while((s32[]{:T(128)}, f32[192,64,64]{0,2,1:T(8,128)}, s32[6,128,4]{1,2,0:T(4,128)}, ...), condition=%wide.region_2.3_spmd.clone.clone, body=%wide.region_0.2_spmd.clone.clone.sunk | while | flops 2020381184 | bytes 46548056 | solution.py:91
  6.2 2.9 %convolution_convert_fusion.4 = bf16[128,16384]{1,0:T(8,128)(2,1)S(1)} fusion(bf16[64,16384]{1,0:T(8,128)(2,1)} %get-tuple-element.320, s32[128]{0:T(128)S(1)} %get-tuple-element.291), kind=kOutput, calls=%fused_computation.3.clone.1 | convolution fusion | flops 270540800 | bytes 6291968 | tf_op jit(solution)/shard_map/while/body/eval_jaxpr/dot_general | solution.py:70
  9.1 3.2 %copy.43 = bf16[16,8,64,256]{3,2,1,0:T(8,128)(2,1)} copy(bf16[16,8,64,256]{3,1,2,0:T(8,128)(2,1)S(1)} %bitcast.89) | data formatting | bytes 8388608 | tf_op jit(solution)/shard_map/while
  12.3 2.8 %gather_fusion = bf16[128,256,64]{1,2,0:T(8,128)(2,1)} fusion(bf16[27,256,64]{1,2,0:T(8,128)(2,1)S(1)} %get-tuple-element.321, s32[1024]{0:T(1024)S(1)} %pad_clamp_fusion.2), kind=kCustom, calls=%fused_computation.clone.clone.1 | custom fusion | bytes 8389120 | tf_op jit(solution)/shard_map/while/body/eval_jaxpr/gather | solution.py:77
  15.1 7.2 %fusion.70 = f32[128,64,64]{2,1,0:T(8,128)} fusion(bf16[128,256,64]{1,2,0:T(8,128)(2,1)} %gather_fusion, bf16[128,64,256]{2,1,0:T(8,128)(2,1)} %bitcast.88, s32[128,64]{1,0:T(8,128)S(1)} %copy.44, pred[128,64]{1,0:T(8,128)(4,1)S(1)} %copy.45), kind=kOutput, calls=%fused_computation.6.clone.1 | convolution fusion | flops 540016640 | bytes 10526720 | tf_op jit(solution)/shard_map/while/body/eval_jaxpr/bvc,bcq->bvq/dot_general | solution.py:78
  22.3 3.8 %copy.46 = f32[128,64,64]{0,2,1:T(8,128)S(1)} copy(f32[128,64,64]{2,1,0:T(8,128)} %fusion.70) | data formatting | bytes 4194304 | tf_op jit(solution)/shard_map/while/body/eval_jaxpr/bvc,bcq->bvq/dot_general | solution.py:78
  26.1 3.8 %select_add_fusion.2 = f32[192,64,64]{0,2,1:T(8,128)} fusion(f32[192,64,64]{0,2,1:T(8,128)} %get-tuple-element.311, f32[128,64,64]{0,2,1:T(8,128)S(1)} %copy.46, pred[]{:T(512)S(6)} %compare.18, s32[128]{0:T(128)S(1)} %get-tuple-element.302), kind=kOutput, calls=%fused_computation.5.clone.1 | convolution fusion | flops 1209556992 | bytes 8389121 | tf_op jit(solution)/shard_map/while/body/eval_jaxpr/dot_general | solution.py:82
  31.1 2.9 %convolution_convert_fusion.4 = bf16[128,16384]{1,0:T(8,128)(2,1)S(1)} fusion(bf16[64,16384]{1,0:T(8,128)(2,1)} %get-tuple-element.320, s32[128]{0:T(128)S(1)} %get-tuple-element.291), kind=kOutput, calls=%fused_computation.3.clone.1 | convolution fusion | flops 270540800 | bytes 6291968 | tf_op jit(solution)/shard_map/while/body/eval_jaxpr/dot_general | solution.py:70
  34.0 3.2 %copy.43 = bf16[16,8,64,256]{3,2,1,0:T(8,128)(2,1)} copy(bf16[16,8,64,256]{3,1,2,0:T(8,128)(2,1)S(1)} %bitcast.89) | data formatting | bytes 8388608 | tf_op jit(solution)/shard_map/while
  37.2 2.8 %gather_fusion = bf16[128,256,64]{1,2,0:T(8,128)(2,1)} fusion(bf16[27,256,64]{1,2,0:T(8,128)(2,1)S(1)} %get-tuple-element.321, s32[1024]{0:T(1024)S(1)} %pad_clamp_fusion.2), kind=kCustom, calls=%fused_computation.clone.clone.1 | custom fusion | bytes 8389120 | tf_op jit(solution)/shard_map/while/body/eval_jaxpr/gather | solution.py:77
  40.0 7.2 %fusion.70 = f32[128,64,64]{2,1,0:T(8,128)} fusion(bf16[128,256,64]{1,2,0:T(8,128)(2,1)} %gather_fusion, bf16[128,64,256]{2,1,0:T(8,128)(2,1)} %bitcast.88, s32[128,64]{1,0:T(8,128)S(1)} %copy.44, pred[128,64]{1,0:T(8,128)(4,1)S(1)} %copy.45), kind=kOutput, calls=%fused_computation.6.clone.1 | convolution fusion | flops 540016640 | bytes 10526720 | tf_op jit(solution)/shard_map/while/body/eval_jaxpr/bvc,bcq->bvq/dot_general | solution.py:78
  47.2 3.8 %copy.46 = f32[128,64,64]{0,2,1:T(8,128)S(1)} copy(f32[128,64,64]{2,1,0:T(8,128)} %fusion.70) | data formatting | bytes 4194304 | tf_op jit(solution)/shard_map/while/body/eval_jaxpr/bvc,bcq->bvq/dot_general | solution.py:78
  51.0 6.0 %select_add_fusion.2 = f32[192,64,64]{0,2,1:T(8,128)} fusion(f32[192,64,64]{0,2,1:T(8,128)} %get-tuple-element.311, f32[128,64,64]{0,2,1:T(8,128)S(1)} %copy.46, pred[]{:T(512)S(6)} %compare.18, s32[128]{0:T(128)S(1)} %get-tuple-element.302), kind=kOutput, calls=%fused_computation.5.clone.1 | convolution fusion | flops 1209556992 | bytes 8389121 | tf_op jit(solution)/shard_map/while/body/eval_jaxpr/dot_general | solution.py:82
  58.3 2.9 %convolution_convert_fusion.4 = bf16[128,16384]{1,0:T(8,128)(2,1)S(1)} fusion(bf16[64,16384]{1,0:T(8,128)(2,1)} %get-tuple-element.320, s32[128]{0:T(128)S(1)} %get-tuple-element.291), kind=kOutput, calls=%fused_computation.3.clone.1 | convolution fusion | flops 270540800 | bytes 6291968 | tf_op jit(solution)/shard_map/while/body/eval_jaxpr/dot_general | solution.py:70
  61.1 3.2 %copy.43 = bf16[16,8,64,256]{3,2,1,0:T(8,128)(2,1)} copy(bf16[16,8,64,256]{3,1,2,0:T(8,128)(2,1)S(1)} %bitcast.89) | data formatting | bytes 8388608 | tf_op jit(solution)/shard_map/while
  64.4 2.8 %gather_fusion = bf16[128,256,64]{1,2,0:T(8,128)(2,1)} fusion(bf16[27,256,64]{1,2,0:T(8,128)(2,1)S(1)} %get-tuple-element.321, s32[1024]{0:T(1024)S(1)} %pad_clamp_fusion.2), kind=kCustom, calls=%fused_computation.clone.clone.1 | custom fusion | bytes 8389120 | tf_op jit(solution)/shard_map/while/body/eval_jaxpr/gather | solution.py:77
  67.1 7.2 %fusion.70 = f32[128,64,64]{2,1,0:T(8,128)} fusion(bf16[128,256,64]{1,2,0:T(8,128)(2,1)} %gather_fusion, bf16[128,64,256]{2,1,0:T(8,128)(2,1)} %bitcast.88, s32[128,64]{1,0:T(8,128)S(1)} %copy.44, pred[128,64]{1,0:T(8,128)(4,1)S(1)} %copy.45), kind=kOutput, calls=%fused_computation.6.clone.1 | convolution fusion | flops 540016640 | bytes 10526720 | tf_op jit(solution)/shard_map/while/body/eval_jaxpr/bvc,bcq->bvq/dot_general | solution.py:78
  74.4 3.8 %copy.46 = f32[128,64,64]{0,2,1:T(8,128)S(1)} copy(f32[128,64,64]{2,1,0:T(8,128)} %fusion.70) | data formatting | bytes 4194304 | tf_op jit(solution)/shard_map/while/body/eval_jaxpr/bvc,bcq->bvq/dot_general | solution.py:78
  78.2 6.0 %select_add_fusion.2 = f32[192,64,64]{0,2,1:T(8,128)} fusion(f32[192,64,64]{0,2,1:T(8,128)} %get-tuple-element.311, f32[128,64,64]{0,2,1:T(8,128)S(1)} %copy.46, pred[]{:T(512)S(6)} %compare.18, s32[128]{0:T(128)S(1)} %get-tuple-element.302), kind=kOutput, calls=%fused_computation.5.clone.1 | convolution fusion | flops 1209556992 | bytes 8389121 | tf_op jit(solution)/shard_map/while/body/eval_jaxpr/dot_general | solution.py:82
  85.4 2.9 %convolution_convert_fusion.4 = bf16[128,16384]{1,0:T(8,128)(2,1)S(1)} fusion(bf16[64,16384]{1,0:T(8,128)(2,1)} %get-tuple-element.320, s32[128]{0:T(128)S(1)} %get-tuple-element.291), kind=kOutput, calls=%fused_computation.3.clone.1 | convolution fusion | flops 270540800 | bytes 6291968 | tf_op jit(solution)/shard_map/while/body/eval_jaxpr/dot_general | solution.py:70
  88.3 3.2 %copy.43 = bf16[16,8,64,256]{3,2,1,0:T(8,128)(2,1)} copy(bf16[16,8,64,256]{3,1,2,0:T(8,128)(2,1)S(1)} %bitcast.89) | data formatting | bytes 8388608 | tf_op jit(solution)/shard_map/while
  91.5 2.8 %gather_fusion = bf16[128,256,64]{1,2,0:T(8,128)(2,1)} fusion(bf16[27,256,64]{1,2,0:T(8,128)(2,1)S(1)} %get-tuple-element.321, s32[1024]{0:T(1024)S(1)} %pad_clamp_fusion.2), kind=kCustom, calls=%fused_computation.clone.clone.1 | custom fusion | bytes 8389120 | tf_op jit(solution)/shard_map/while/body/eval_jaxpr/gather | solution.py:77
  94.3 7.2 %fusion.70 = f32[128,64,64]{2,1,0:T(8,128)} fusion(bf16[128,256,64]{1,2,0:T(8,128)(2,1)} %gather_fusion, bf16[128,64,256]{2,1,0:T(8,128)(2,1)} %bitcast.88, s32[128,64]{1,0:T(8,128)S(1)} %copy.44, pred[128,64]{1,0:T(8,128)(4,1)S(1)} %copy.45), kind=kOutput, calls=%fused_computation.6.clone.1 | convolution fusion | flops 540016640 | bytes 10526720 | tf_op jit(solution)/shard_map/while/body/eval_jaxpr/bvc,bcq->bvq/dot_general | solution.py:78
  101.5 3.8 %copy.46 = f32[128,64,64]{0,2,1:T(8,128)S(1)} copy(f32[128,64,64]{2,1,0:T(8,128)} %fusion.70) | data formatting | bytes 4194304 | tf_op jit(solution)/shard_map/while/body/eval_jaxpr/bvc,bcq->bvq/dot_general | solution.py:78
  105.3 6.0 %select_add_fusion.2 = f32[192,64,64]{0,2,1:T(8,128)} fusion(f32[192,64,64]{0,2,1:T(8,128)} %get-tuple-element.311, f32[128,64,64]{0,2,1:T(8,128)S(1)} %copy.46, pred[]{:T(512)S(6)} %compare.18, s32[128]{0:T(128)S(1)} %get-tuple-element.302), kind=kOutput, calls=%fused_computation.5.clone.1 | convolution fusion | flops 1209556992 | bytes 8389121 | tf_op jit(solution)/shard_map/while/body/eval_jaxpr/dot_general | solution.py:82
  112.5 2.9 %convolution_convert_fusion.4 = bf16[128,16384]{1,0:T(8,128)(2,1)S(1)} fusion(bf16[64,16384]{1,0:T(8,128)(2,1)} %get-tuple-element.320, s32[128]{0:T(128)S(1)} %get-tuple-element.291), kind=kOutput, calls=%fused_computation.3.clone.1 | convolution fusion | flops 270540800 | bytes 6291968 | tf_op jit(solution)/shard_map/while/body/eval_jaxpr/dot_general | solution.py:70
  115.4 3.2 %copy.43 = bf16[16,8,64,256]{3,2,1,0:T(8,128)(2,1)} copy(bf16[16,8,64,256]{3,1,2,0:T(8,128)(2,1)S(1)} %bitcast.89) | data formatting | bytes 8388608 | tf_op jit(solution)/shard_map/while
  118.6 2.8 %gather_fusion = bf16[128,256,64]{1,2,0:T(8,128)(2,1)} fusion(bf16[27,256,64]{1,2,0:T(8,128)(2,1)S(1)} %get-tuple-element.321, s32[1024]{0:T(1024)S(1)} %pad_clamp_fusion.2), kind=kCustom, calls=%fused_computation.clone.clone.1 | custom fusion | bytes 8389120 | tf_op jit(solution)/shard_map/while/body/eval_jaxpr/gather | solution.py:77
  121.4 7.2 %fusion.70 = f32[128,64,64]{2,1,0:T(8,128)} fusion(bf16[128,256,64]{1,2,0:T(8,128)(2,1)} %gather_fusion, bf16[128,64,256]{2,1,0:T(8,128)(2,1)} %bitcast.88, s32[128,64]{1,0:T(8,128)S(1)} %copy.44, pred[128,64]{1,0:T(8,128)(4,1)S(1)} %copy.45), kind=kOutput, calls=%fused_computation.6.clone.1 | convolution fusion | flops 540016640 | bytes 10526720 | tf_op jit(solution)/shard_map/while/body/eval_jaxpr/bvc,bcq->bvq/dot_general | solution.py:78
  128.6 3.8 %copy.46 = f32[128,64,64]{0,2,1:T(8,128)S(1)} copy(f32[128,64,64]{2,1,0:T(8,128)} %fusion.70) | data formatting | bytes 4194304 | tf_op jit(solution)/shard_map/while/body/eval_jaxpr/bvc,bcq->bvq/dot_general | solution.py:78
  132.4 6.0 %select_add_fusion.2 = f32[192,64,64]{0,2,1:T(8,128)} fusion(f32[192,64,64]{0,2,1:T(8,128)} %get-tuple-element.311, f32[128,64,64]{0,2,1:T(8,128)S(1)} %copy.46, pred[]{:T(512)S(6)} %compare.18, s32[128]{0:T(128)S(1)} %get-tuple-element.302), kind=kOutput, calls=%fused_computation.5.clone.1 | convolution fusion | flops 1209556992 | bytes 8389121 | tf_op jit(solution)/shard_map/while/body/eval_jaxpr/dot_general | solution.py:82
  139.6 2.9 %convolution_convert_fusion.4 = bf16[128,16384]{1,0:T(8,128)(2,1)S(1)} fusion(bf16[64,16384]{1,0:T(8,128)(2,1)} %get-tuple-element.320, s32[128]{0:T(128)S(1)} %get-tuple-element.291), kind=kOutput, calls=%fused_computation.3.clone.1 | convolution fusion | flops 270540800 | bytes 6291968 | tf_op jit(solution)/shard_map/while/body/eval_jaxpr/dot_general | solution.py:70
  142.5 3.2 %copy.43 = bf16[16,8,64,256]{3,2,1,0:T(8,128)(2,1)} copy(bf16[16,8,64,256]{3,1,2,0:T(8,128)(2,1)S(1)} %bitcast.89) | data formatting | bytes 8388608 | tf_op jit(solution)/shard_map/while
  148.5 7.2 %fusion.70 = f32[128,64,64]{2,1,0:T(8,128)} fusion(bf16[128,256,64]{1,2,0:T(8,128)(2,1)} %gather_fusion, bf16[128,64,256]{2,1,0:T(8,128)(2,1)} %bitcast.88, s32[128,64]{1,0:T(8,128)S(1)} %copy.44, pred[128,64]{1,0:T(8,128)(4,1)S(1)} %copy.45), kind=kOutput, calls=%fused_computation.6.clone.1 | convolution fusion | flops 540016640 | bytes 10526720 | tf_op jit(solution)/shard_map/while/body/eval_jaxpr/bvc,bcq->bvq/dot_general | solution.py:78
  155.7 3.8 %copy.46 = f32[128,64,64]{0,2,1:T(8,128)S(1)} copy(f32[128,64,64]{2,1,0:T(8,128)} %fusion.70) | data formatting | bytes 4194304 | tf_op jit(solution)/shard_map/while/body/eval_jaxpr/bvc,bcq->bvq/dot_general | solution.py:78
  159.5 6.0 %select_add_fusion.2 = f32[192,64,64]{0,2,1:T(8,128)} fusion(f32[192,64,64]{0,2,1:T(8,128)} %get-tuple-element.311, f32[128,64,64]{0,2,1:T(8,128)S(1)} %copy.46, pred[]{:T(512)S(6)} %compare.18, s32[128]{0:T(128)S(1)} %get-tuple-element.302), kind=kOutput, calls=%fused_computation.5.clone.1 | convolution fusion | flops 1209556992 | bytes 8389121 | tf_op jit(solution)/shard_map/while/body/eval_jaxpr/dot_general | solution.py:82
  165.5 6.2 %copy.31 = bf16[192,64,64]{2,1,0:T(8,128)(2,1)} copy(f32[192,64,64]{0,2,1:T(8,128)} %get-tuple-element.164) | data formatting | bytes 4718592 | tf_op jit(solution)/shard_map/while | solution.py:91
  174.3 5.5 %collective-permute-start = (bf16[16,64,64]{2,1,0:T(8,128)(2,1)}, bf16[16,64,64]{2,1,0:T(8,128)(2,1)}, u32[]{:S(2)}, u32[]{:S(2)}) collective-permute-start(bf16[16,64,64]{2,1,0:T(8,128)(2,1)} %get-tuple-element.243), channel_id=1, source_target_pairs={{0,4},{4,8},{8,12},{12,16},{16,20},{20,24},{24,28},{1,5},{5,9},{9,... | collective-permute-start | bytes 393224 | tf_op jit(solution)/shard_map/ppermute | solution.py:12
  179.8 3.5 %collective-permute-start.1 = (bf16[16,64,64]{2,1,0:T(8,128)(2,1)}, bf16[16,64,64]{2,1,0:T(8,128)(2,1)}, u32[]{:S(2)}, u32[]{:S(2)}) collective-permute-start(bf16[16,64,64]{2,1,0:T(8,128)(2,1)} %get-tuple-element.242), channel_id=1, source_target_pairs={{0,8},{4,12},{8,16},{12,20},{16,24},{20,28},{1,9},{5,13},{9,17},{1... | collective-permute-start | bytes 393224 | tf_op jit(solution)/shard_map/ppermute | solution.py:12
  183.4 4.5 %collective-permute-start.2 = (bf16[16,64,64]{2,1,0:T(8,128)(2,1)}, bf16[16,64,64]{2,1,0:T(8,128)(2,1)}, u32[]{:S(2)}, u32[]{:S(2)}) collective-permute-start(bf16[16,64,64]{2,1,0:T(8,128)(2,1)} %get-tuple-element.241), channel_id=1, source_target_pairs={{0,12},{4,16},{8,20},{12,24},{16,28},{1,13},{5,17},{9,21},{13,25},... | collective-permute-start | bytes 393224 | tf_op jit(solution)/shard_map/ppermute | solution.py:12
  207.9 6.2 %collective-permute-done.6 = bf16[16,64,64]{2,1,0:T(8,128)(2,1)S(1)} collective-permute-done((bf16[16,64,64]{2,1,0:T(8,128)(2,1)S(1)}, bf16[16,64,64]{2,1,0:T(8,128)(2,1)S(1)}, u32[]{:S(2)}, u32[]{:S(2)}) %collective-permute-start.6) | collective-permute-done | bytes 131104 | tf_op jit(solution)/shard_map/ppermute | solution.py:12
  214.8 14.5 %collective-permute-done.7 = bf16[16,64,64]{2,1,0:T(8,128)(2,1)S(1)} collective-permute-done((bf16[16,64,64]{2,1,0:T(8,128)(2,1)S(1)}, bf16[16,64,64]{2,1,0:T(8,128)(2,1)S(1)}, u32[]{:S(2)}, u32[]{:S(2)}) %collective-permute-start.7) | collective-permute-done | bytes 131104 | tf_op jit(solution)/shard_map/ppermute | solution.py:12
  230.1 3.3 %reshape.246 = bf16[128,4096]{1,0:T(8,128)(2,1)S(1)} reshape(bf16[8,16,64,64]{3,2,1,0:T(8,128)(2,1)} %bitcast_dynamic-update-slice_fusion) | data formatting | bytes 2097152 | tf_op jit(solution)/shard_map/reshape | solution.py:97
  234.7 3.7 %multiply_reduce_fusion = (f32[64,64]{0,1:T(8,128)S(1)}, f32[64,64,64]{0,2,1:T(8,128)}) fusion(bf16[64,64,128]{2,1,0:T(8,128)(2,1)} %bitcast.93, s32[128]{0:T(128)S(1)} %bitcast.98, f32[192,64,64]{0,2,1:T(8,128)} %get-tuple-element.164), kind=kOutput, calls=%fused_computation.71 | convolution fusion | flops 67899392 | bytes 3162624 | tf_op jit(solution)/shard_map/dot_general | solution.py:99
  238.4 10.3 %psum.7 = f32[64,64]{0,1:T(8,128)S(1)} all-reduce(f32[64,64]{0,1:T(8,128)S(1)} %get-tuple-element.244), channel_id=1, replica_groups=mesh['tiles'=8,'chan'=4] {'chan'}, use_global_device_ids=true, to_apply=%region_4.5 | all-reduce | flops 4096 | bytes 32768 | tf_op jit(solution)/shard_map/psum | solution.py:103
  253.0 3.4 %all-to-all-start = ((bf16[8,2,2048]{2,1,0:T(2,128)(2,1)}), bf16[8,2,2048]{2,1,0:T(2,128)(2,1)S(1)}, u32[]{:S(2)}, u32[]{:S(2)}) async-start(bf16[8,2,2048]{2,1,0:T(2,128)(2,1)} %reshape.271), calls=%async_computation | async-start | bytes 131072 | tf_op jit(solution)/shard_map/all_to_all | solution.py:118
  258.7 4.5 %all-to-all-done = bf16[8,2,2048]{2,1,0:T(2,128)(2,1)S(1)} async-done(((bf16[8,2,2048]{2,1,0:T(2,128)(2,1)}), bf16[8,2,2048]{2,1,0:T(2,128)(2,1)S(1)}, u32[]{:S(2)}, u32[]{:S(2)}) %all-to-all-start) | async-done | bytes 65568 | tf_op jit(solution)/shard_map/all_to_all | solution.py:118
  (137 shorter events, 43.2 us)
Async XLA Ops:
  0.6 4.3 %copy-start = (bf16[27,256,64]{1,2,0:T(8,128)(2,1)S(1)}, bf16[27,256,64]{1,2,0:T(8,128)(2,1)}, u32[]{:S(2)}) copy-start(bf16[27,256,64]{1,2,0:T(8,128)(2,1)} %param.10) | copy-start | bytes 2654212
  171.7 19.5 %copy-start.1 = (bf16[64,64,256]{2,1,0:T(8,128)(2,1)S(1)}, bf16[64,64,256]{2,1,0:T(8,128)(2,1)}, u32[]{:S(2)}) copy-start(bf16[64,64,256]{2,1,0:T(8,128)(2,1)} %param.9) | copy-start | bytes 6291460
  174.3 20.4 %collective-permute-start = (bf16[16,64,64]{2,1,0:T(8,128)(2,1)}, bf16[16,64,64]{2,1,0:T(8,128)(2,1)}, u32[]{:S(2)}, u32[]{:S(2)}) collective-permute-start(bf16[16,64,64]{2,1,0:T(8,128)(2,1)} %get-tuple-element.243), channel_id=1, source_target_pairs={{0,4},{4,8},{8,12},{12,16},{16,20},{20,24},{24,28},{1,5},{5,9},{9,... | collective-permute-start | bytes 393224 | tf_op jit(solution)/shard_map/ppermute | solution.py:12
  179.8 17.9 %collective-permute-start.1 = (bf16[16,64,64]{2,1,0:T(8,128)(2,1)}, bf16[16,64,64]{2,1,0:T(8,128)(2,1)}, u32[]{:S(2)}, u32[]{:S(2)}) collective-permute-start(bf16[16,64,64]{2,1,0:T(8,128)(2,1)} %get-tuple-element.242), channel_id=1, source_target_pairs={{0,8},{4,12},{8,16},{12,20},{16,24},{20,28},{1,9},{5,13},{9,17},{1... | collective-permute-start | bytes 393224 | tf_op jit(solution)/shard_map/ppermute | solution.py:12
  183.4 17.3 %collective-permute-start.2 = (bf16[16,64,64]{2,1,0:T(8,128)(2,1)}, bf16[16,64,64]{2,1,0:T(8,128)(2,1)}, u32[]{:S(2)}, u32[]{:S(2)}) collective-permute-start(bf16[16,64,64]{2,1,0:T(8,128)(2,1)} %get-tuple-element.241), channel_id=1, source_target_pairs={{0,12},{4,16},{8,20},{12,24},{16,28},{1,13},{5,17},{9,21},{13,25},... | collective-permute-start | bytes 393224 | tf_op jit(solution)/shard_map/ppermute | solution.py:12
  187.8 16.0 %collective-permute-start.3 = (bf16[16,64,64]{2,1,0:T(8,128)(2,1)S(1)}, bf16[16,64,64]{2,1,0:T(8,128)(2,1)}, u32[]{:S(2)}, u32[]{:S(2)}) collective-permute-start(bf16[16,64,64]{2,1,0:T(8,128)(2,1)S(1)} %get-tuple-element.240), channel_id=1, source_target_pairs={{0,16},{4,20},{8,24},{12,28},{1,17},{5,21},{9,25},{13,29},{2,18},{... | collective-permute-start | bytes 393224 | tf_op jit(solution)/shard_map/ppermute | solution.py:12
  189.8 15.7 %collective-permute-start.4 = (bf16[16,64,64]{2,1,0:T(8,128)(2,1)S(1)}, bf16[16,64,64]{2,1,0:T(8,128)(2,1)}, u32[]{:S(2)}, u32[]{:S(2)}) collective-permute-start(bf16[16,64,64]{2,1,0:T(8,128)(2,1)S(1)} %get-tuple-element.239), channel_id=1, source_target_pairs={{4,0},{8,4},{12,8},{16,12},{20,16},{24,20},{28,24},{5,1},{9,5},{13... | collective-permute-start | bytes 393224 | tf_op jit(solution)/shard_map/ppermute | solution.py:12
  191.1 3.6 %copy-start.5 = (bf16[64]{0:T(256)(128)(2,1)S(1)}, bf16[64]{0:T(256)(128)(2,1)}, u32[]{:S(2)}) copy-start(bf16[64]{0:T(256)(128)(2,1)} %param.11) | copy-start | bytes 388
  194.7 12.4 %collective-permute-start.5 = (bf16[16,64,64]{2,1,0:T(8,128)(2,1)S(1)}, bf16[16,64,64]{2,1,0:T(8,128)(2,1)S(1)}, u32[]{:S(2)}, u32[]{:S(2)}) collective-permute-start(bf16[16,64,64]{2,1,0:T(8,128)(2,1)S(1)} %get-tuple-element.238), channel_id=1, source_target_pairs={{8,0},{12,4},{16,8},{20,12},{24,16},{28,20},{9,1},{13,5},{17,9},{2... | collective-permute-start | bytes 393224 | tf_op jit(solution)/shard_map/ppermute | solution.py:12
  197.7 16.3 %collective-permute-start.6 = (bf16[16,64,64]{2,1,0:T(8,128)(2,1)S(1)}, bf16[16,64,64]{2,1,0:T(8,128)(2,1)S(1)}, u32[]{:S(2)}, u32[]{:S(2)}) collective-permute-start(bf16[16,64,64]{2,1,0:T(8,128)(2,1)S(1)} %get-tuple-element.237), channel_id=1, source_target_pairs={{12,0},{16,4},{20,8},{24,12},{28,16},{13,1},{17,5},{21,9},{25,13},... | collective-permute-start | bytes 393224 | tf_op jit(solution)/shard_map/ppermute | solution.py:12
  200.7 28.6 %collective-permute-start.7 = (bf16[16,64,64]{2,1,0:T(8,128)(2,1)S(1)}, bf16[16,64,64]{2,1,0:T(8,128)(2,1)S(1)}, u32[]{:S(2)}, u32[]{:S(2)}) collective-permute-start(bf16[16,64,64]{2,1,0:T(8,128)(2,1)S(1)} %get-tuple-element.236), channel_id=1, source_target_pairs={{16,0},{20,4},{24,8},{28,12},{17,1},{21,5},{25,9},{29,13},{18,2},{... | collective-permute-start | bytes 393224 | tf_op jit(solution)/shard_map/ppermute | solution.py:12
  230.1 4.6 %copy-start.4 = (s32[1,128]{1,0:T(1,128)S(1)}, s32[1,128]{1,0:T(1,128)}, u32[]{:S(2)}) copy-start(s32[1,128]{1,0:T(1,128)} %param.13) | copy-start | bytes 1540
  251.1 0.8 copy-start.2
  251.3 12.2 %copy-start.3 = (s32[1,8]{1,0:T(1,128)S(1)}, s32[1,8]{1,0:T(1,128)}, u32[]{:S(2)}) copy-start(s32[1,8]{1,0:T(1,128)} %param.15) | copy-start | bytes 100
  253.0 10.2 %all-to-all-start = ((bf16[8,2,2048]{2,1,0:T(2,128)(2,1)}), bf16[8,2,2048]{2,1,0:T(2,128)(2,1)S(1)}, u32[]{:S(2)}, u32[]{:S(2)}) async-start(bf16[8,2,2048]{2,1,0:T(2,128)(2,1)} %reshape.271), calls=%async_computation | async-start | bytes 131072 | tf_op jit(solution)/shard_map/all_to_all | solution.py:118
where the time goes:
time: 266 us; the launch traced here: 265 us
  local copies, waits for them, and re-layouts  101 us (38%)
  matrix products  98.2 us (37%)
  waiting for transfers between devices  25.2 us (9%)
  starting transfers between devices  24.2 us (9%)
  blocking collectives  10.3 us (4%)
  other arithmetic  4.43 us (2%)
    dot_general x6, matrix products, step_rules(): jnp.einsum('bvc,bcq->bvq', chosen, kernels, preferred_element_type=jnp.fl...  43.3 us
    dot_general x6, matrix products, step_rules(): jnp.dot(target_hot, partial_out.reshape(group.shape[0], 64 * quarter), pr...  33.6 us
    dot_general x6, local copies, waits for them, and re-layouts, step_rules(): jnp.einsum('bvc,bcq->bvq', chosen, kernels, preferred_element_type=jnp.fl...  22.7 us
    ppermute x8, starting transfers between devices, from_behind(): return lax.ppermute(block, axis, route)  20.8 us
    ppermute x8, waiting for transfers between devices, from_behind(): return lax.ppermute(block, axis, route)  20.7 us
    unnamed x24, local copies, waits for them, and re-layouts  19.5 us
    while x6, local copies, waits for them, and re-layouts  19.3 us
    dot_general x6, matrix products, step_rules(): jnp.dot(source_hot, flat_features, preferred_element_type=jnp.float32)  17.3 us
  transfers between devices with their start and end apart: 9, of which 3 were waited for; matrix products, arithmetic and copies ran while one was open for 6% of the time, Pallas kernels for 0%

commit v1 on v0

--- a/solution.py
+++ b/solution.py
@@ -100,7 +100,7 @@
         tile_count, 64, quarter
     )
     convolved = totals[:tile_count] + gathered_in
-    squares = lax.psum(jnp.sum(convolved * convolved, axis=-1), "chan")
+    squares = jnp.sum(lax.all_gather(jnp.sum(convolved * convolved, axis=-1), "chan"), axis=0)
     mean_square = squares[:, :, None] / channels
     hidden = jax.nn.silu(gain.astype(jnp.float32) * convolved * lax.rsqrt(mean_square + epsilon))
     skip_features = (own_part.astype(jnp.float32) + hidden).astype(jnp.bfloat16)

time: 266 us -> 255 us (0.959)
  local copies, waits for them, and re-layouts: 101 us -> 92.1 us
  blocking collectives: 10.3 us -> 5.42 us
  waiting for transfers between devices: 25.2 us -> 29.9 us
    psum x1 -> x0, blocking collectives: 10.3 us -> none  [body(): squares = lax.psum(jnp.sum(convolved * convolved, axis=-1), 'chan')]
    all_gather x0 -> x1, blocking collectives: none -> 5.42 us  [body(): lax.all_gather(jnp.sum(convolved * convolved, axis=-1), 'chan')]
    ppermute x8, waiting for transfers between devices: 20.7 us -> 25.4 us  [from_behind(): return lax.ppermute(block, axis, route)]
    unnamed x24, local copies, waits for them, and re-layouts: 19.5 us -> 15.2 us
  transfers between devices with their start and end apart: 9 -> 9, of which waited for: 3 -> 4; matrix products, arithmetic and copies ran while one was open for 6% -> 4% of each run, Pallas kernels for 0% -> 0%
where the time goes in v1:
time: 255 us; the launch traced here: 254 us
  matrix products  96.9 us (38%)
  local copies, waits for them, and re-layouts  92.1 us (36%)
  waiting for transfers between devices  29.9 us (12%)
  starting transfers between devices  24.2 us (9%)
  blocking collectives  5.42 us (2%)
  other arithmetic  4.08 us (2%)
    dot_general x6, matrix products, step_rules(): jnp.einsum('bvc,bcq->bvq', chosen, kernels, preferred_element_type=jnp.fl...  43.3 us
    dot_general x6, matrix products, step_rules(): jnp.dot(target_hot, partial_out.reshape(group.shape[0], 64 * quarter), pr...  33.6 us
    ppermute x8, waiting for transfers between devices, from_behind(): return lax.ppermute(block, axis, route)  25.4 us
    dot_general x6, local copies, waits for them, and re-layouts, step_rules(): jnp.einsum('bvc,bcq->bvq', chosen, kernels, preferred_element_type=jnp.fl...  22.7 us
    ppermute x8, starting transfers between devices, from_behind(): return lax.ppermute(block, axis, route)  20.8 us
    while x6, local copies, waits for them, and re-layouts  19.3 us
    dot_general x6, matrix products, step_rules(): jnp.dot(source_hot, flat_features, preferred_element_type=jnp.float32)  17.3 us
    gather x6, local copies, waits for them, and re-layouts, step_rules(): kernels = weights[jnp.minimum(group[:, 1], 26)]  16.6 us
  transfers between devices with their start and end apart: 9, of which 4 were waited for; matrix products, arithmetic and copies ran while one was open for 4% of the time, Pallas kernels for 0%

profile of v1, /device:TPU:0, one launch (start us, length us, event | category | flops | bytes accessed | tf_op | source)
XLA Modules:
  0.0 254.0 jit_solution(3885448647540461879)
XLA Ops:
  0.7 4.3 %copy.59 = bf16[8,8,64,256]{3,1,2,0:T(8,128)(2,1)} copy(bf16[8,8,64,256]{3,2,1,0:T(8,128)(2,1)} %bitcast.92) | data formatting | bytes 4194304
  4.9 160.6 %while.16 = (s32[]{:T(128)}, f32[192,64,64]{0,2,1:T(8,128)}, s32[6,128,4]{1,2,0:T(4,128)}, bf16[64,16384]{1,0:T(8,128)(2,1)}, bf16[27,256,64]{1,2,0:T(8,128)(2,1)S(1)}, /*index=5*/s32[]{:T(128)}, s32[]{:T(128)}) while((s32[]{:T(128)}, f32[192,64,64]{0,2,1:T(8,128)}, s32[6,128,4]{1,2,0:T(4,128)}, ...), condition=%wide.region_2.3_spmd.clone.clone, body=%wide.region_0.2_spmd.clone.clone.sunk | while | flops 2020381184 | bytes 46548056 | solution.py:91
  6.2 2.9 %convolution_convert_fusion.4 = bf16[128,16384]{1,0:T(8,128)(2,1)S(1)} fusion(bf16[64,16384]{1,0:T(8,128)(2,1)} %get-tuple-element.324, s32[128]{0:T(128)S(1)} %get-tuple-element.295), kind=kOutput, calls=%fused_computation.3.clone.1 | convolution fusion | flops 270540800 | bytes 6291968 | tf_op jit(solution)/shard_map/while/body/eval_jaxpr/dot_general | solution.py:70
  9.1 3.2 %copy.64 = bf16[16,8,64,256]{3,2,1,0:T(8,128)(2,1)} copy(bf16[16,8,64,256]{3,1,2,0:T(8,128)(2,1)S(1)} %bitcast.90) | data formatting | bytes 8388608 | tf_op jit(solution)/shard_map/while
  12.3 2.8 %gather_fusion = bf16[128,256,64]{1,2,0:T(8,128)(2,1)} fusion(bf16[27,256,64]{1,2,0:T(8,128)(2,1)S(1)} %get-tuple-element.325, s32[1024]{0:T(1024)S(1)} %pad_clamp_fusion.2), kind=kCustom, calls=%fused_computation.clone.clone.1 | custom fusion | bytes 8389120 | tf_op jit(solution)/shard_map/while/body/eval_jaxpr/gather | solution.py:77
  15.1 7.2 %fusion.70 = f32[128,64,64]{2,1,0:T(8,128)} fusion(bf16[128,256,64]{1,2,0:T(8,128)(2,1)} %gather_fusion, bf16[128,64,256]{2,1,0:T(8,128)(2,1)} %bitcast.89, s32[128,64]{1,0:T(8,128)S(1)} %copy.65, pred[128,64]{1,0:T(8,128)(4,1)S(1)} %copy.66), kind=kOutput, calls=%fused_computation.6.clone.1 | convolution fusion | flops 540016640 | bytes 10526720 | tf_op jit(solution)/shard_map/while/body/eval_jaxpr/bvc,bcq->bvq/dot_general | solution.py:78
  22.3 3.8 %copy.67 = f32[128,64,64]{0,2,1:T(8,128)S(1)} copy(f32[128,64,64]{2,1,0:T(8,128)} %fusion.70) | data formatting | bytes 4194304 | tf_op jit(solution)/shard_map/while/body/eval_jaxpr/bvc,bcq->bvq/dot_general | solution.py:78
  26.1 3.8 %select_add_fusion.2 = f32[192,64,64]{0,2,1:T(8,128)} fusion(f32[192,64,64]{0,2,1:T(8,128)} %get-tuple-element.315, f32[128,64,64]{0,2,1:T(8,128)S(1)} %copy.67, pred[]{:T(512)S(6)} %compare.18, s32[128]{0:T(128)S(1)} %get-tuple-element.306), kind=kOutput, calls=%fused_computation.5.clone.1 | convolution fusion | flops 1209556992 | bytes 8389121 | tf_op jit(solution)/shard_map/while/body/eval_jaxpr/dot_general | solution.py:82
  31.1 2.9 %convolution_convert_fusion.4 = bf16[128,16384]{1,0:T(8,128)(2,1)S(1)} fusion(bf16[64,16384]{1,0:T(8,128)(2,1)} %get-tuple-element.324, s32[128]{0:T(128)S(1)} %get-tuple-element.295), kind=kOutput, calls=%fused_computation.3.clone.1 | convolution fusion | flops 270540800 | bytes 6291968 | tf_op jit(solution)/shard_map/while/body/eval_jaxpr/dot_general | solution.py:70
  34.0 3.2 %copy.64 = bf16[16,8,64,256]{3,2,1,0:T(8,128)(2,1)} copy(bf16[16,8,64,256]{3,1,2,0:T(8,128)(2,1)S(1)} %bitcast.90) | data formatting | bytes 8388608 | tf_op jit(solution)/shard_map/while
  37.2 2.8 %gather_fusion = bf16[128,256,64]{1,2,0:T(8,128)(2,1)} fusion(bf16[27,256,64]{1,2,0:T(8,128)(2,1)S(1)} %get-tuple-element.325, s32[1024]{0:T(1024)S(1)} %pad_clamp_fusion.2), kind=kCustom, calls=%fused_computation.clone.clone.1 | custom fusion | bytes 8389120 | tf_op jit(solution)/shard_map/while/body/eval_jaxpr/gather | solution.py:77
  40.0 7.2 %fusion.70 = f32[128,64,64]{2,1,0:T(8,128)} fusion(bf16[128,256,64]{1,2,0:T(8,128)(2,1)} %gather_fusion, bf16[128,64,256]{2,1,0:T(8,128)(2,1)} %bitcast.89, s32[128,64]{1,0:T(8,128)S(1)} %copy.65, pred[128,64]{1,0:T(8,128)(4,1)S(1)} %copy.66), kind=kOutput, calls=%fused_computation.6.clone.1 | convolution fusion | flops 540016640 | bytes 10526720 | tf_op jit(solution)/shard_map/while/body/eval_jaxpr/bvc,bcq->bvq/dot_general | solution.py:78
  47.2 3.8 %copy.67 = f32[128,64,64]{0,2,1:T(8,128)S(1)} copy(f32[128,64,64]{2,1,0:T(8,128)} %fusion.70) | data formatting | bytes 4194304 | tf_op jit(solution)/shard_map/while/body/eval_jaxpr/bvc,bcq->bvq/dot_general | solution.py:78
  51.0 6.0 %select_add_fusion.2 = f32[192,64,64]{0,2,1:T(8,128)} fusion(f32[192,64,64]{0,2,1:T(8,128)} %get-tuple-element.315, f32[128,64,64]{0,2,1:T(8,128)S(1)} %copy.67, pred[]{:T(512)S(6)} %compare.18, s32[128]{0:T(128)S(1)} %get-tuple-element.306), kind=kOutput, calls=%fused_computation.5.clone.1 | convolution fusion | flops 1209556992 | bytes 8389121 | tf_op jit(solution)/shard_map/while/body/eval_jaxpr/dot_general | solution.py:82
  58.3 2.9 %convolution_convert_fusion.4 = bf16[128,16384]{1,0:T(8,128)(2,1)S(1)} fusion(bf16[64,16384]{1,0:T(8,128)(2,1)} %get-tuple-element.324, s32[128]{0:T(128)S(1)} %get-tuple-element.295), kind=kOutput, calls=%fused_computation.3.clone.1 | convolution fusion | flops 270540800 | bytes 6291968 | tf_op jit(solution)/shard_map/while/body/eval_jaxpr/dot_general | solution.py:70
  61.1 3.2 %copy.64 = bf16[16,8,64,256]{3,2,1,0:T(8,128)(2,1)} copy(bf16[16,8,64,256]{3,1,2,0:T(8,128)(2,1)S(1)} %bitcast.90) | data formatting | bytes 8388608 | tf_op jit(solution)/shard_map/while
  64.4 2.8 %gather_fusion = bf16[128,256,64]{1,2,0:T(8,128)(2,1)} fusion(bf16[27,256,64]{1,2,0:T(8,128)(2,1)S(1)} %get-tuple-element.325, s32[1024]{0:T(1024)S(1)} %pad_clamp_fusion.2), kind=kCustom, calls=%fused_computation.clone.clone.1 | custom fusion | bytes 8389120 | tf_op jit(solution)/shard_map/while/body/eval_jaxpr/gather | solution.py:77
  67.1 7.2 %fusion.70 = f32[128,64,64]{2,1,0:T(8,128)} fusion(bf16[128,256,64]{1,2,0:T(8,128)(2,1)} %gather_fusion, bf16[128,64,256]{2,1,0:T(8,128)(2,1)} %bitcast.89, s32[128,64]{1,0:T(8,128)S(1)} %copy.65, pred[128,64]{1,0:T(8,128)(4,1)S(1)} %copy.66), kind=kOutput, calls=%fused_computation.6.clone.1 | convolution fusion | flops 540016640 | bytes 10526720 | tf_op jit(solution)/shard_map/while/body/eval_jaxpr/bvc,bcq->bvq/dot_general | solution.py:78
  74.4 3.8 %copy.67 = f32[128,64,64]{0,2,1:T(8,128)S(1)} copy(f32[128,64,64]{2,1,0:T(8,128)} %fusion.70) | data formatting | bytes 4194304 | tf_op jit(solution)/shard_map/while/body/eval_jaxpr/bvc,bcq->bvq/dot_general | solution.py:78
  78.2 6.0 %select_add_fusion.2 = f32[192,64,64]{0,2,1:T(8,128)} fusion(f32[192,64,64]{0,2,1:T(8,128)} %get-tuple-element.315, f32[128,64,64]{0,2,1:T(8,128)S(1)} %copy.67, pred[]{:T(512)S(6)} %compare.18, s32[128]{0:T(128)S(1)} %get-tuple-element.306), kind=kOutput, calls=%fused_computation.5.clone.1 | convolution fusion | flops 1209556992 | bytes 8389121 | tf_op jit(solution)/shard_map/while/body/eval_jaxpr/dot_general | solution.py:82
  85.4 2.9 %convolution_convert_fusion.4 = bf16[128,16384]{1,0:T(8,128)(2,1)S(1)} fusion(bf16[64,16384]{1,0:T(8,128)(2,1)} %get-tuple-element.324, s32[128]{0:T(128)S(1)} %get-tuple-element.295), kind=kOutput, calls=%fused_computation.3.clone.1 | convolution fusion | flops 270540800 | bytes 6291968 | tf_op jit(solution)/shard_map/while/body/eval_jaxpr/dot_general | solution.py:70
  88.3 3.2 %copy.64 = bf16[16,8,64,256]{3,2,1,0:T(8,128)(2,1)} copy(bf16[16,8,64,256]{3,1,2,0:T(8,128)(2,1)S(1)} %bitcast.90) | data formatting | bytes 8388608 | tf_op jit(solution)/shard_map/while
  91.5 2.8 %gather_fusion = bf16[128,256,64]{1,2,0:T(8,128)(2,1)} fusion(bf16[27,256,64]{1,2,0:T(8,128)(2,1)S(1)} %get-tuple-element.325, s32[1024]{0:T(1024)S(1)} %pad_clamp_fusion.2), kind=kCustom, calls=%fused_computation.clone.clone.1 | custom fusion | bytes 8389120 | tf_op jit(solution)/shard_map/while/body/eval_jaxpr/gather | solution.py:77
  94.3 7.2 %fusion.70 = f32[128,64,64]{2,1,0:T(8,128)} fusion(bf16[128,256,64]{1,2,0:T(8,128)(2,1)} %gather_fusion, bf16[128,64,256]{2,1,0:T(8,128)(2,1)} %bitcast.89, s32[128,64]{1,0:T(8,128)S(1)} %copy.65, pred[128,64]{1,0:T(8,128)(4,1)S(1)} %copy.66), kind=kOutput, calls=%fused_computation.6.clone.1 | convolution fusion | flops 540016640 | bytes 10526720 | tf_op jit(solution)/shard_map/while/body/eval_jaxpr/bvc,bcq->bvq/dot_general | solution.py:78
  101.5 3.8 %copy.67 = f32[128,64,64]{0,2,1:T(8,128)S(1)} copy(f32[128,64,64]{2,1,0:T(8,128)} %fusion.70) | data formatting | bytes 4194304 | tf_op jit(solution)/shard_map/while/body/eval_jaxpr/bvc,bcq->bvq/dot_general | solution.py:78
  105.3 6.0 %select_add_fusion.2 = f32[192,64,64]{0,2,1:T(8,128)} fusion(f32[192,64,64]{0,2,1:T(8,128)} %get-tuple-element.315, f32[128,64,64]{0,2,1:T(8,128)S(1)} %copy.67, pred[]{:T(512)S(6)} %compare.18, s32[128]{0:T(128)S(1)} %get-tuple-element.306), kind=kOutput, calls=%fused_computation.5.clone.1 | convolution fusion | flops 1209556992 | bytes 8389121 | tf_op jit(solution)/shard_map/while/body/eval_jaxpr/dot_general | solution.py:82
  112.5 2.9 %convolution_convert_fusion.4 = bf16[128,16384]{1,0:T(8,128)(2,1)S(1)} fusion(bf16[64,16384]{1,0:T(8,128)(2,1)} %get-tuple-element.324, s32[128]{0:T(128)S(1)} %get-tuple-element.295), kind=kOutput, calls=%fused_computation.3.clone.1 | convolution fusion | flops 270540800 | bytes 6291968 | tf_op jit(solution)/shard_map/while/body/eval_jaxpr/dot_general | solution.py:70
  115.4 3.2 %copy.64 = bf16[16,8,64,256]{3,2,1,0:T(8,128)(2,1)} copy(bf16[16,8,64,256]{3,1,2,0:T(8,128)(2,1)S(1)} %bitcast.90) | data formatting | bytes 8388608 | tf_op jit(solution)/shard_map/while
  118.6 2.8 %gather_fusion = bf16[128,256,64]{1,2,0:T(8,128)(2,1)} fusion(bf16[27,256,64]{1,2,0:T(8,128)(2,1)S(1)} %get-tuple-element.325, s32[1024]{0:T(1024)S(1)} %pad_clamp_fusion.2), kind=kCustom, calls=%fused_computation.clone.clone.1 | custom fusion | bytes 8389120 | tf_op jit(solution)/shard_map/while/body/eval_jaxpr/gather | solution.py:77
  121.4 7.2 %fusion.70 = f32[128,64,64]{2,1,0:T(8,128)} fusion(bf16[128,256,64]{1,2,0:T(8,128)(2,1)} %gather_fusion, bf16[128,64,256]{2,1,0:T(8,128)(2,1)} %bitcast.89, s32[128,64]{1,0:T(8,128)S(1)} %copy.65, pred[128,64]{1,0:T(8,128)(4,1)S(1)} %copy.66), kind=kOutput, calls=%fused_computation.6.clone.1 | convolution fusion | flops 540016640 | bytes 10526720 | tf_op jit(solution)/shard_map/while/body/eval_jaxpr/bvc,bcq->bvq/dot_general | solution.py:78
  128.6 3.8 %copy.67 = f32[128,64,64]{0,2,1:T(8,128)S(1)} copy(f32[128,64,64]{2,1,0:T(8,128)} %fusion.70) | data formatting | bytes 4194304 | tf_op jit(solution)/shard_map/while/body/eval_jaxpr/bvc,bcq->bvq/dot_general | solution.py:78
  132.4 6.0 %select_add_fusion.2 = f32[192,64,64]{0,2,1:T(8,128)} fusion(f32[192,64,64]{0,2,1:T(8,128)} %get-tuple-element.315, f32[128,64,64]{0,2,1:T(8,128)S(1)} %copy.67, pred[]{:T(512)S(6)} %compare.18, s32[128]{0:T(128)S(1)} %get-tuple-element.306), kind=kOutput, calls=%fused_computation.5.clone.1 | convolution fusion | flops 1209556992 | bytes 8389121 | tf_op jit(solution)/shard_map/while/body/eval_jaxpr/dot_general | solution.py:82
  139.6 2.9 %convolution_convert_fusion.4 = bf16[128,16384]{1,0:T(8,128)(2,1)S(1)} fusion(bf16[64,16384]{1,0:T(8,128)(2,1)} %get-tuple-element.324, s32[128]{0:T(128)S(1)} %get-tuple-element.295), kind=kOutput, calls=%fused_computation.3.clone.1 | convolution fusion | flops 270540800 | bytes 6291968 | tf_op jit(solution)/shard_map/while/body/eval_jaxpr/dot_general | solution.py:70
  142.5 3.2 %copy.64 = bf16[16,8,64,256]{3,2,1,0:T(8,128)(2,1)} copy(bf16[16,8,64,256]{3,1,2,0:T(8,128)(2,1)S(1)} %bitcast.90) | data formatting | bytes 8388608 | tf_op jit(solution)/shard_map/while
  145.7 2.8 %gather_fusion = bf16[128,256,64]{1,2,0:T(8,128)(2,1)} fusion(bf16[27,256,64]{1,2,0:T(8,128)(2,1)S(1)} %get-tuple-element.325, s32[1024]{0:T(1024)S(1)} %pad_clamp_fusion.2), kind=kCustom, calls=%fused_computation.clone.clone.1 | custom fusion | bytes 8389120 | tf_op jit(solution)/shard_map/while/body/eval_jaxpr/gather | solution.py:77
  148.5 7.2 %fusion.70 = f32[128,64,64]{2,1,0:T(8,128)} fusion(bf16[128,256,64]{1,2,0:T(8,128)(2,1)} %gather_fusion, bf16[128,64,256]{2,1,0:T(8,128)(2,1)} %bitcast.89, s32[128,64]{1,0:T(8,128)S(1)} %copy.65, pred[128,64]{1,0:T(8,128)(4,1)S(1)} %copy.66), kind=kOutput, calls=%fused_computation.6.clone.1 | convolution fusion | flops 540016640 | bytes 10526720 | tf_op jit(solution)/shard_map/while/body/eval_jaxpr/bvc,bcq->bvq/dot_general | solution.py:78
  155.7 3.8 %copy.67 = f32[128,64,64]{0,2,1:T(8,128)S(1)} copy(f32[128,64,64]{2,1,0:T(8,128)} %fusion.70) | data formatting | bytes 4194304 | tf_op jit(solution)/shard_map/while/body/eval_jaxpr/bvc,bcq->bvq/dot_general | solution.py:78
  159.5 6.0 %select_add_fusion.2 = f32[192,64,64]{0,2,1:T(8,128)} fusion(f32[192,64,64]{0,2,1:T(8,128)} %get-tuple-element.315, f32[128,64,64]{0,2,1:T(8,128)S(1)} %copy.67, pred[]{:T(512)S(6)} %compare.18, s32[128]{0:T(128)S(1)} %get-tuple-element.306), kind=kOutput, calls=%fused_computation.5.clone.1 | convolution fusion | flops 1209556992 | bytes 8389121 | tf_op jit(solution)/shard_map/while/body/eval_jaxpr/dot_general | solution.py:82
  165.5 5.2 %copy.50 = bf16[192,64,64]{2,1,0:T(8,128)(2,1)S(1)} copy(f32[192,64,64]{0,2,1:T(8,128)} %get-tuple-element.164) | data formatting | bytes 4718592 | tf_op jit(solution)/shard_map/while | solution.py:91
  171.9 4.8 %collective-permute-start = (bf16[16,64,64]{2,1,0:T(8,128)(2,1)}, bf16[16,64,64]{2,1,0:T(8,128)(2,1)S(1)}, u32[]{:S(2)}, u32[]{:S(2)}) collective-permute-start(bf16[16,64,64]{2,1,0:T(8,128)(2,1)} %get-tuple-element.247), channel_id=1, source_target_pairs={{0,4},{4,8},{8,12},{12,16},{16,20},{20,24},{24,28},{1,5},{5,9},{9,... | collective-permute-start | bytes 393224 | tf_op jit(solution)/shard_map/ppermute | solution.py:12
  176.8 4.2 %collective-permute-start.1 = (bf16[16,64,64]{2,1,0:T(8,128)(2,1)}, bf16[16,64,64]{2,1,0:T(8,128)(2,1)}, u32[]{:S(2)}, u32[]{:S(2)}) collective-permute-start(bf16[16,64,64]{2,1,0:T(8,128)(2,1)} %get-tuple-element.246), channel_id=1, source_target_pairs={{0,8},{4,12},{8,16},{12,20},{16,24},{20,28},{1,9},{5,13},{9,17},{1... | collective-permute-start | bytes 393224 | tf_op jit(solution)/shard_map/ppermute | solution.py:12
  181.0 4.5 %collective-permute-start.2 = (bf16[16,64,64]{2,1,0:T(8,128)(2,1)}, bf16[16,64,64]{2,1,0:T(8,128)(2,1)}, u32[]{:S(2)}, u32[]{:S(2)}) collective-permute-start(bf16[16,64,64]{2,1,0:T(8,128)(2,1)} %get-tuple-element.245), channel_id=1, source_target_pairs={{0,12},{4,16},{8,20},{12,24},{16,28},{1,13},{5,17},{9,21},{13,25},... | collective-permute-start | bytes 393224 | tf_op jit(solution)/shard_map/ppermute | solution.py:12
  204.3 8.2 %collective-permute-done.6 = bf16[16,64,64]{2,1,0:T(8,128)(2,1)S(1)} collective-permute-done((bf16[16,64,64]{2,1,0:T(8,128)(2,1)}, bf16[16,64,64]{2,1,0:T(8,128)(2,1)S(1)}, u32[]{:S(2)}, u32[]{:S(2)}) %collective-permute-start.6) | collective-permute-done | bytes 131104 | tf_op jit(solution)/shard_map/ppermute | solution.py:12
  212.6 14.9 %collective-permute-done.7 = bf16[16,64,64]{2,1,0:T(8,128)(2,1)S(1)} collective-permute-done((bf16[16,64,64]{2,1,0:T(8,128)(2,1)S(1)}, bf16[16,64,64]{2,1,0:T(8,128)(2,1)S(1)}, u32[]{:S(2)}, u32[]{:S(2)}) %collective-permute-start.7) | collective-permute-done | bytes 131104 | tf_op jit(solution)/shard_map/ppermute | solution.py:12
  230.6 2.4 multiply_reduce_fusion
  233.0 5.4 %all-gather = f32[256,64]{1,0:T(8,128)S(1)} all-gather(f32[64,64]{1,0:T(8,128)S(1)} %copy.52), channel_id=2, replica_groups=mesh['tiles'=8,'chan'=4] {'chan'}, dimensions={0}, use_global_device_ids=true | all-gather | bytes 81920 | tf_op jit(solution)/shard_map/all_gather | solution.py:103
  242.5 3.4 %all-to-all-start = ((bf16[8,2,2048]{2,1,0:T(2,128)(2,1)}), bf16[8,2,2048]{2,1,0:T(2,128)(2,1)S(1)}, u32[]{:S(2)}, u32[]{:S(2)}) async-start(bf16[8,2,2048]{2,1,0:T(2,128)(2,1)} %reshape.276), calls=%async_computation | async-start | bytes 131072 | tf_op jit(solution)/shard_map/all_to_all | solution.py:118
  248.2 4.5 %all-to-all-done = bf16[8,2,2048]{2,1,0:T(2,128)(2,1)S(1)} async-done(((bf16[8,2,2048]{2,1,0:T(2,128)(2,1)}), bf16[8,2,2048]{2,1,0:T(2,128)(2,1)S(1)}, u32[]{:S(2)}, u32[]{:S(2)}) %all-to-all-start) | async-done | bytes 65568 | tf_op jit(solution)/shard_map/all_to_all | solution.py:118
  (140 shorter events, 37.9 us)
Async XLA Ops:
  0.6 4.3 %copy-start = (bf16[27,256,64]{1,2,0:T(8,128)(2,1)S(1)}, bf16[27,256,64]{1,2,0:T(8,128)(2,1)}, u32[]{:S(2)}) copy-start(bf16[27,256,64]{1,2,0:T(8,128)(2,1)} %param.10) | copy-start | bytes 2654212
  171.9 20.4 %collective-permute-start = (bf16[16,64,64]{2,1,0:T(8,128)(2,1)}, bf16[16,64,64]{2,1,0:T(8,128)(2,1)S(1)}, u32[]{:S(2)}, u32[]{:S(2)}) collective-permute-start(bf16[16,64,64]{2,1,0:T(8,128)(2,1)} %get-tuple-element.247), channel_id=1, source_target_pairs={{0,4},{4,8},{8,12},{12,16},{16,20},{20,24},{24,28},{1,5},{5,9},{9,... | collective-permute-start | bytes 393224 | tf_op jit(solution)/shard_map/ppermute | solution.py:12
  176.8 18.5 %collective-permute-start.1 = (bf16[16,64,64]{2,1,0:T(8,128)(2,1)}, bf16[16,64,64]{2,1,0:T(8,128)(2,1)}, u32[]{:S(2)}, u32[]{:S(2)}) collective-permute-start(bf16[16,64,64]{2,1,0:T(8,128)(2,1)} %get-tuple-element.246), channel_id=1, source_target_pairs={{0,8},{4,12},{8,16},{12,20},{16,24},{20,28},{1,9},{5,13},{9,17},{1... | collective-permute-start | bytes 393224 | tf_op jit(solution)/shard_map/ppermute | solution.py:12
  181.0 16.6 %collective-permute-start.2 = (bf16[16,64,64]{2,1,0:T(8,128)(2,1)}, bf16[16,64,64]{2,1,0:T(8,128)(2,1)}, u32[]{:S(2)}, u32[]{:S(2)}) collective-permute-start(bf16[16,64,64]{2,1,0:T(8,128)(2,1)} %get-tuple-element.245), channel_id=1, source_target_pairs={{0,12},{4,16},{8,20},{12,24},{16,28},{1,13},{5,17},{9,21},{13,25},... | collective-permute-start | bytes 393224 | tf_op jit(solution)/shard_map/ppermute | solution.py:12
  185.4 14.6 %collective-permute-start.3 = (bf16[16,64,64]{2,1,0:T(8,128)(2,1)}, bf16[16,64,64]{2,1,0:T(8,128)(2,1)}, u32[]{:S(2)}, u32[]{:S(2)}) collective-permute-start(bf16[16,64,64]{2,1,0:T(8,128)(2,1)} %get-tuple-element.244), channel_id=1, source_target_pairs={{0,16},{4,20},{8,24},{12,28},{1,17},{5,21},{9,25},{13,29},{2,18},{... | collective-permute-start | bytes 393224 | tf_op jit(solution)/shard_map/ppermute | solution.py:12
  187.4 13.6 %collective-permute-start.4 = (bf16[16,64,64]{2,1,0:T(8,128)(2,1)}, bf16[16,64,64]{2,1,0:T(8,128)(2,1)}, u32[]{:S(2)}, u32[]{:S(2)}) collective-permute-start(bf16[16,64,64]{2,1,0:T(8,128)(2,1)} %get-tuple-element.243), channel_id=1, source_target_pairs={{4,0},{8,4},{12,8},{16,12},{20,16},{24,20},{28,24},{5,1},{9,5},{13... | collective-permute-start | bytes 393224 | tf_op jit(solution)/shard_map/ppermute | solution.py:12
  188.7 3.6 %copy-start.5 = (bf16[64]{0:T(256)(128)(2,1)S(1)}, bf16[64]{0:T(256)(128)(2,1)}, u32[]{:S(2)}) copy-start(bf16[64]{0:T(256)(128)(2,1)} %param.11) | copy-start | bytes 388
  192.3 0.7 copy-start.1
  193.0 11.3 %collective-permute-start.5 = (bf16[16,64,64]{2,1,0:T(8,128)(2,1)}, bf16[16,64,64]{2,1,0:T(8,128)(2,1)S(1)}, u32[]{:S(2)}, u32[]{:S(2)}) collective-permute-start(bf16[16,64,64]{2,1,0:T(8,128)(2,1)} %get-tuple-element.242), channel_id=1, source_target_pairs={{8,0},{12,4},{16,8},{20,12},{24,16},{28,20},{9,1},{13,5},{17,9},{2... | collective-permute-start | bytes 393224 | tf_op jit(solution)/shard_map/ppermute | solution.py:12
  195.3 17.3 %collective-permute-start.6 = (bf16[16,64,64]{2,1,0:T(8,128)(2,1)}, bf16[16,64,64]{2,1,0:T(8,128)(2,1)S(1)}, u32[]{:S(2)}, u32[]{:S(2)}) collective-permute-start(bf16[16,64,64]{2,1,0:T(8,128)(2,1)} %get-tuple-element.241), channel_id=1, source_target_pairs={{12,0},{16,4},{20,8},{24,12},{28,16},{13,1},{17,5},{21,9},{25,13},... | collective-permute-start | bytes 393224 | tf_op jit(solution)/shard_map/ppermute | solution.py:12
  197.6 29.9 %collective-permute-start.7 = (bf16[16,64,64]{2,1,0:T(8,128)(2,1)S(1)}, bf16[16,64,64]{2,1,0:T(8,128)(2,1)S(1)}, u32[]{:S(2)}, u32[]{:S(2)}) collective-permute-start(bf16[16,64,64]{2,1,0:T(8,128)(2,1)S(1)} %get-tuple-element.240), channel_id=1, source_target_pairs={{16,0},{20,4},{24,8},{28,12},{17,1},{21,5},{25,9},{29,13},{18,2},{... | collective-permute-start | bytes 393224 | tf_op jit(solution)/shard_map/ppermute | solution.py:12
  227.5 3.0 %copy-start.4 = (s32[1,128]{1,0:T(1,128)S(1)}, s32[1,128]{1,0:T(1,128)}, u32[]{:S(2)}) copy-start(s32[1,128]{1,0:T(1,128)} %param.13) | copy-start | bytes 1540
  240.6 0.8 copy-start.2
  240.8 12.2 %copy-start.3 = (s32[1,8]{1,0:T(1,128)S(1)}, s32[1,8]{1,0:T(1,128)}, u32[]{:S(2)}) copy-start(s32[1,8]{1,0:T(1,128)} %param.15) | copy-start | bytes 100
  242.5 10.2 %all-to-all-start = ((bf16[8,2,2048]{2,1,0:T(2,128)(2,1)}), bf16[8,2,2048]{2,1,0:T(2,128)(2,1)S(1)}, u32[]{:S(2)}, u32[]{:S(2)}) async-start(bf16[8,2,2048]{2,1,0:T(2,128)(2,1)} %reshape.276), calls=%async_computation | async-start | bytes 131072 | tf_op jit(solution)/shard_map/all_to_all | solution.py:118
